TPU v7x, 512 devices: a whole 4x4x16 slice. The times are simulated.
512 devices in a mesh: band: 8 (over y, core), exp: 64 (over x, z).
Axes of the slice: x: 4, y: 4, z: 16, core: 2. Of those that a mesh axis runs over, the one named last changes fastest.
Arguments:
- exposure: float32 [524288, 512], P(('band', 'exp')), parts along dimension 0, may hold values from -8 to 8, as said below
- psf_taps: bfloat16 [512, 15], P(('band', 'exp')), parts along dimension 0, may hold values from -1.5 to 1.5
- col_warp: bfloat16 [262144, 512], P(('band', 'exp')), parts along dimension 0, may hold values from -0.25 to 0.25
- row_warp: bfloat16 [262144, 1024], P(('band', 'exp')), parts along dimension 0, may hold values from -0.1875 to 0.1875
- row_patch: int32 [262144, 1], P(('band', 'exp')), parts along dimension 0, may hold values from 0 to 63; in each aligned block of 512 rows (0 to 511, 512 to 1023, ...) at most 16 rows name the same one
- row_prow: int32 [262144], P(('band', 'exp')), parts along dimension 0, may hold values from 0 to 31
- owner_map: int32 [512], P('band'), parts along dimension 0, may hold values from 0 to 63, each once
Outputs:
- coadd: float32 [16384, 512], P(('band', 'exp')), parts along dimension 0
There are 8 independent parts, one for each index of `band`. A program takes and returns all parts, laid end to end along the dimension named above; each array names one. Nothing has to cross between parts.
Inputs may be any that keep to these rules, and one draw needn't show every extreme that they name: `row_patch`: the 512 resampled rows of one exposure piece (aligned blocks) name any one patch at most 16 times, a bound that some block reaches. `exposure`: each piece carries a background level per block of 128 columns on top of the sky noise.
All inputs are finite; a program needn't handle non-finite values.
Results may differ from a plain program's by a relative error of at most 0.0051.
Values sent between devices are 32-bit elements; how exact they have to be, the bound alone decides.
A program may use at most 64 MiB of HBM per device.

v0:
```python
import jax
import jax.numpy as jnp
from jax import lax
from jax.sharding import PartitionSpec as P

STRIP = 16
TAPS = 15
PATCH_ROWS = 32


def extended(block, sides, width):
    for axis, dim in sides:
        count = lax.axis_size(axis)
        forward = [(i, i + 1) for i in range(count - 1)]
        forward.append((count - 1, 0))
        backward = [(target, source) for source, target in forward]
        low = lax.ppermute(
            lax.slice_in_dim(block, block.shape[dim] - width, None, axis=dim), axis, forward
        )
        high = lax.ppermute(lax.slice_in_dim(block, 0, width, axis=dim), axis, backward)
        block = jnp.concatenate([low, block, high], axis=dim)
    return block


def make_band(taps, width):
    half = (TAPS - 1) // 2
    rows_idx = jnp.arange(width, dtype=jnp.int32)[:, None]
    cols_idx = jnp.arange(width, dtype=jnp.int32)[None, :]
    offset = rows_idx - cols_idx + half
    band = jnp.zeros((width, width), jnp.bfloat16)
    for tap in range(TAPS):
        band = jnp.where(offset == tap, taps[tap], band)
    return band


def block_mean(strip, width):
    return jnp.mean(strip.reshape(STRIP, width // 128, 128), axis=(0, 2))


def on_device(exposure, psf_taps, col_warp, row_warp, row_patch, row_prow, owner_map):
    rows, width = exposure.shape
    out_rows = row_warp.shape[0]
    devices = lax.axis_size("exp")
    padded = extended(exposure, (("exp", 0),), STRIP)
    prev_last = padded[:STRIP]
    next_first = padded[rows + STRIP :]
    off_next = block_mean(exposure[rows - STRIP :] - next_first, width)
    off_prev = block_mean(prev_last - exposure[:STRIP], width)
    shift = jnp.repeat(-0.5 * off_next + 0.5 * off_prev, 128)
    corrected = (exposure + shift[None, :]).astype(jnp.bfloat16)
    band = make_band(psf_taps[0], width)
    matched = jnp.dot(corrected, band, preferred_element_type=jnp.float32).astype(jnp.bfloat16)
    warped_cols = jnp.dot(matched, col_warp, preferred_element_type=jnp.float32).astype(
        jnp.bfloat16
    )
    warped = jnp.dot(row_warp, warped_cols, preferred_element_type=jnp.float32)
    slot_ids = jnp.arange(devices, dtype=jnp.int32)
    slot_of = jnp.sum(
        jnp.where(owner_map[:, None] == slot_ids[None, :], slot_ids[:, None], 0), axis=0
    )
    patch = row_patch[:, 0]
    dest = jnp.sum(jnp.where(patch[:, None] == slot_ids[None, :], slot_of[None, :], 0), axis=1)
    key = dest * PATCH_ROWS + row_prow
    count = PATCH_ROWS * lax.axis_size("exp")
    local = key
    inside = (local >= 0) & (local < count)
    local = jnp.where(inside, local, count)
    sums = lax.psum_scatter(
        jax.ops.segment_sum(warped, local, num_segments=count + 1)[:count],
        "exp",
        scatter_dimension=0,
        tiled=True,
    )
    ones_term = jax.ops.segment_sum(
        jnp.ones((out_rows,), jnp.float32), key, num_segments=devices * PATCH_ROWS
    )
    counts = lax.psum_scatter(ones_term, "exp", scatter_dimension=0, tiled=True)
    return sums / jnp.maximum(counts, 1.0)[:, None]


def solution(mesh):
    placed = (
        P(("band", "exp"), None),
        P(("band", "exp"), None),
        P(("band", "exp"), None),
        P(("band", "exp"), None),
        P(("band", "exp"), None),
        P(("band", "exp")),
        P("band"),
    )
    return jax.shard_map(
        on_device, mesh=mesh, in_specs=placed, out_specs=P(("band", "exp"), None), check_vma=False
    )
```

profile of v0, /device:TPU:24, one launch (start us, length us, event | category | flops | bytes accessed | tf_op | source)
XLA Modules:
  0.0 747.3 jit_solution(721905083756580263)
XLA Ops:
  6.5 0.9 fusion.132
  7.4 3.8 collective-permute-start.1
  11.2 11.7 %collective-permute-start = (f32[16,512]{1,0:T(8,128)S(1)}, f32[16,512]{1,0:T(8,128)S(1)}, u32[]{:S(2)}, u32[]{:S(2)}) collective-permute-start(f32[16,512]{1,0:T(8,128)S(1)} %get-tuple-element.10), channel_id=1, source_target_pairs={{1,0},{2,1},{3,2},{4,3},{5,4},{6,5},{7,6},{8,7},{9,8},{10,9},{11,1... | collective-permute-start | bytes 98312 | tf_op jit(solution)/shard_map/ppermute | solution.py:20
  22.9 0.7 select_reduce_fusion.1
  23.7 0.8 select_reduce_fusion
  24.5 0.7 and_select_fusion
  25.1 1.9 fusion.133
  27.1 0.0 collective-permute-done.1
  27.1 0.0 collective-permute-done
  27.1 0.8 subtract_reduce_fusion.1
  27.9 0.1 bitcast_reduce_fusion
  28.0 0.1 broadcast_bitcast_fusion
  28.1 13.4 %convolution_convert_fusion = bf16[1024,512]{1,0:T(8,128)(2,1)} fusion(bf16[512,512]{1,0:T(8,128)(2,1)} %param.9, f32[1024,512]{1,0:T(8,128)} %param.7, f32[512]{0:T(512)S(1)} %broadcast_bitcast_fusion, bf16[]{:T(256)} %bitcast.18, bf16[]{:T(256)} %bitcast.17, bf16[]{:T(256)} %bitcast.16, bf16[]{:T(256)} %bitcast.15, bf16[]{:T(256)} %bitcast.14, ...), kind=kOutput, calls=%fused_computation.5 | convolution fusion | flops 1084227584 | bytes 3672094 | tf_op jit(solution)/shard_map/dot_general | solution.py:53
  41.6 2.0 convolution_bitcast_fusion
  43.5 0.3 copy.10
  43.9 5.7 scatter_custom_fusion
  49.6 4.6 slice.89
  54.2 0.0 reduce-scatter.2.cloned.1.call-update
  54.2 1.3 dynamic-slice
  56.2 3.3 scatter_custom_fusion.1
  59.4 143.7 %all-reduce = f32[2048]{0:T(1024)S(1)} all-reduce(f32[2048]{0:T(1024)S(1)} %scatter_custom_fusion.1), channel_id=3, replica_groups=mesh['band'=8,'exp'=64] {'exp'}, use_global_device_ids=true, to_apply=%region_9.10.clone | all-reduce | flops 2048 | bytes 16384
  203.1 0.1 dynamic-slice_maximum_fusion
  203.2 535.7 %reduce-scatter.2.cloned.1.call-done = f32[32,512]{1,0:T(8,128)} async-done(((f32[2048,512]{1,0:T(8,128)}), f32[32,512]{1,0:T(8,128)}) %reduce-scatter.2.cloned.1.call-update) | async-done | bytes 65552 | tf_op jit(solution)/shard_map/reduce_scatter | solution.py:68
  738.9 1.5 broadcast_divide_fusion
  (5 shorter events, 0.0 us)
Async XLA Ops:
  6.5 35.0 %copy-start = (bf16[512,1024]{1,0:T(8,128)(2,1)S(1)}, bf16[512,1024]{1,0:T(8,128)(2,1)}, u32[]{:S(2)}) copy-start(bf16[512,1024]{1,0:T(8,128)(2,1)} %param.10) | copy-start | bytes 3145732
  6.5 732.3 %reduce-scatter.2.cloned.1.call-start = ((), (), s32[]{:S(2)}) async-start(), calls=%async_computation.1 | async-start | bytes 4259840 | tf_op jit(solution)/shard_map/reduce_scatter | solution.py:68
  7.4 19.6 %collective-permute-start.1 = (f32[16,512]{1,0:T(8,128)S(1)}, f32[16,512]{1,0:T(8,128)S(1)}, u32[]{:S(2)}, u32[]{:S(2)}) collective-permute-start(f32[16,512]{1,0:T(8,128)S(1)} %get-tuple-element.9), channel_id=1, source_target_pairs={{0,1},{1,2},{2,3},{3,4},{4,5},{5,6},{6,7},{7,8},{8,9},{9,10},{10,1... | collective-permute-start | bytes 98312 | tf_op jit(solution)/shard_map/ppermute | solution.py:17
  11.2 15.8 %collective-permute-start = (f32[16,512]{1,0:T(8,128)S(1)}, f32[16,512]{1,0:T(8,128)S(1)}, u32[]{:S(2)}, u32[]{:S(2)}) collective-permute-start(f32[16,512]{1,0:T(8,128)S(1)} %get-tuple-element.10), channel_id=1, source_target_pairs={{1,0},{2,1},{3,2},{4,3},{5,4},{6,5},{7,6},{8,7},{9,8},{10,9},{11,1... | collective-permute-start | bytes 98312 | tf_op jit(solution)/shard_map/ppermute | solution.py:20
Sparse Core Ops, SparseCore 0:
  54.4 684.4 reduce-scatter.1
where the time goes:
time: 748 us; the launch traced here: 747 us
  waiting for transfers between devices  536 us (72%)
  blocking collectives  144 us (19%)
  starting transfers between devices  15.5 us (2%)
  matrix products  15.4 us (2%)
  between operations  14.1 us (2%)
  other arithmetic  13.8 us (2%)
  local copies, waits for them, and re-layouts  9.05 us (1%)
    reduce_scatter x1, waiting for transfers between devices, on_device(): lax.psum_scatter(jax.ops.segment_sum(warped, local, num_segments=count +...  536 us
    unnamed x1, blocking collectives  144 us
  transfers between devices with their start and end apart: 3, of which 1 were waited for; matrix products, arithmetic and copies ran while one was open for 1% of the time, Pallas kernels for 0%

commit v1 on v0

v1 whole, which is shorter than its diff:
```python
import functools

import jax
import jax.numpy as jnp
from jax import lax
from jax.experimental import pallas as pl
from jax.experimental.pallas import tpu as pltpu
from jax.sharding import PartitionSpec as P

F32, BF16, I32 = jnp.float32, jnp.bfloat16, jnp.int32
MESH = pl.DeviceIdType.MESH

STRIP = 16
TAPS = 15
PROWS = 32
CAP = 16
NX, NZ = 4, 16
W, R, RO = 512, 1024, 512
LANES = 128

NA = 2
NB = 2
RB = 1
BROWS = NX * PROWS // RB
ORDER = (
    ("b", 1), ("b", 2), ("x", 0), ("a0", 0), ("b", 3), ("a0", 1), ("b", 4), ("x", 1), ("a1", 0), ("a0", 2), ("a1", 1), ("b", 5),
    ("a0", 3), ("a1", 2), ("b", 6), ("a0", 4), ("a1", 3), ("b", 7), ("a0", 5), ("a1", 4), ("bx", 0), ("a0", 6), ("a1", 5),
    ("a0", 7), ("a1", 6), ("a1", 7),
)


def nt(a, b):
    return lax.dot_general(a, b, (((1,), (1,)), ((), ())), preferred_element_type=F32)


def mm(a, b):
    return jnp.dot(a, b, preferred_element_type=F32)


def iota(shape, dim):
    return lax.broadcasted_iota(I32, shape, dim)


def kernel(
    expo, taps, cw_hbm, rw_hbm, patch, prow, owner, out,
    ex, cw, rw, mat, tbuf, wbuf, sel, pack, halo_out, halo_in, cnt,
    bown, bring, bsend, brecv, xsend, xrecv, msend, mrecv, acc, aring,
    in_sem, hs, hr, bs, br, bxs, bxr, xs, xr, ms, mr, az, ar,
):
    e = lax.axis_index("exp")
    x, z = e // NZ, lax.rem(e, NZ)

    def dev(i):
        return {"exp": i}

    def at_z(d):
        return x * NZ + lax.rem(z + d + NZ, NZ)

    def at_x(d):
        return lax.rem(x + d + NX, NX) * NZ + z

    def remote(src, dst, s, r, target):
        return pltpu.make_async_remote_copy(
            src_ref=src, dst_ref=dst, send_sem=s, recv_sem=r, device_id=dev(target), device_id_type=MESH
        )

    nxt, prv = lax.rem(e + 1, NX * NZ), lax.rem(e + NX * NZ - 1, NX * NZ)

    quarter = R // 4
    loads = []
    for k, q in enumerate((0, 3, 1, 2)):
        rows = pl.ds(q * quarter, quarter)
        loads.append(pltpu.make_async_copy(expo.at[rows], ex.at[rows], in_sem.at[k]))
    loads.append(pltpu.make_async_copy(cw_hbm, cw, in_sem.at[4]))
    loads.append(pltpu.make_async_copy(rw_hbm, rw, in_sem.at[5]))
    for load in loads:
        load.start()

    barrier = pltpu.get_barrier_semaphore()
    peers = (at_z(1), at_z(-1), at_x(1), at_x(2), at_x(3), nxt, prv)
    for peer in peers:
        pl.semaphore_signal(barrier, inc=1, device_id=dev(peer), device_id_type=MESH)

    eye = iota((64, 64), 0) == iota((64, 64), 1)
    owner_col = jnp.sum(jnp.where(eye, jnp.broadcast_to(owner[...], (64, 64)), 0), axis=1, keepdims=True)
    own_of = owner_col == patch[...]
    slot_id = iota((64, RO), 0)
    dest = jnp.sum(jnp.where(own_of, slot_id, 0), axis=0, keepdims=True)
    dest_x, dest_z = dest // NZ, lax.rem(dest, NZ)
    in_z = dest_x * PROWS + prow[...]
    key = dest_z * (NX * PROWS) + in_z

    one_hot = jnp.where(own_of, 1.0, 0.0)
    before = jnp.where(iota((RO, RO), 0) < iota((RO, RO), 1), 1.0, 0.0).astype(BF16)
    earlier = mm(one_hot.astype(BF16), before)
    rank = jnp.sum(one_hot * earlier, axis=0, keepdims=True).astype(I32)
    slot = dest_x * (NZ * CAP) + dest_z * CAP + rank

    loads[0].wait()
    loads[1].wait()

    def means(rows):
        total = jnp.sum(ex[rows, :], axis=0, keepdims=True)
        parts = [
            jnp.broadcast_to(
                jnp.sum(total[:, b * LANES : (b + 1) * LANES], axis=1, keepdims=True) * (1.0 / (STRIP * LANES)), (1, LANES)
            )
            for b in range(W // LANES)
        ]
        return jnp.concatenate(parts, axis=1)

    first, last = means(slice(0, STRIP)), means(slice(R - STRIP, R))
    halo_out[0] = jnp.broadcast_to(first, (8, W))
    halo_out[1] = jnp.broadcast_to(last, (8, W))

    prow_row = jnp.broadcast_to((prow[...] + 1).astype(F32), (8, RO)).astype(BF16)
    for g in range(NX):
        place = jnp.where(iota((NZ * CAP, RO), 0) == slot - g * (NZ * CAP), 1.0, 0.0).astype(BF16)
        pack[g] = place
        msend[g] = nt(prow_row, place)

    pl.semaphore_wait(barrier, len(peers))
    halo = [
        remote(halo_out.at[0], halo_in.at[0], hs.at[0], hr.at[0], prv),
        remote(halo_out.at[1], halo_in.at[1], hs.at[1], hr.at[1], nxt),
    ]
    for copy in halo:
        copy.start()
    meta = []
    for k in (1, 2, 3):
        g = lax.rem(x + k, NX)
        meta.append(remote(msend.at[g], mrecv.at[k - 1], ms.at[k - 1], mr.at[k - 1], at_x(k)))
        meta[-1].start()

    oz = jnp.where(iota((NZ, RO), 0) == dest_z, 1.0, 0.0).astype(BF16)
    oq = jnp.where(iota((LANES, RO), 0) == in_z, 1.0, 0.0).astype(BF16)
    cnt[...] = nt(oz, oq)

    @pl.loop(0, NZ)
    def _(d):
        sel[pl.ds(pl.multiple_of(d * LANES, LANES), LANES), :] = jnp.where(
            iota((LANES, RO), 0) == key - d * LANES, 1.0, 0.0
        ).astype(BF16)

    offset = iota((LANES, 3 * LANES), 0) - iota((LANES, 3 * LANES), 1) + (LANES + (TAPS - 1) // 2)
    band = jnp.zeros((LANES, 3 * LANES), F32)
    tap = taps[...].astype(F32)
    for t in range(TAPS):
        band = jnp.where(offset == t, jnp.broadcast_to(tap[:, t : t + 1], (LANES, 3 * LANES)), band)
    band = band.astype(BF16)
    loads[4].wait()
    for b in range(W // LANES):
        low, high = max(b - 1, 0), min(b + 2, W // LANES)
        strip = band[:, (low - b + 1) * LANES : (high - b + 1) * LANES]
        mat[b * LANES : (b + 1) * LANES, :] = mm(strip, cw[low * LANES : high * LANES, :]).astype(BF16)

    loads[2].wait()
    loads[3].wait()
    loads[5].wait()
    for copy in halo:
        copy.wait_recv()
    off_next = last - halo_in[0][0:1]
    off_prev = halo_in[1][0:1] - first
    shift = -0.5 * off_next + 0.5 * off_prev

    @pl.loop(0, 4)
    def _(q):
        rows = pl.ds(pl.multiple_of(q * quarter, quarter), quarter)
        corrected = (ex[rows, :] + shift).astype(BF16)
        tbuf[rows, :] = mm(corrected, mat[...]).astype(BF16)

    @pl.loop(0, 2)
    def _(q):
        rows = pl.ds(pl.multiple_of(q * 256, 256), 256)
        wbuf[rows, :] = mm(rw[rows, :], tbuf[...]).astype(BF16)

    started = []

    def start(copy):
        copy.start()
        started.append(copy)

    def send_packed(c):
        cols = slice(c * LANES, (c + 1) * LANES)
        for k in (2, 1, 3, 0):
            g = lax.rem(x + k, NX)
            xsend[c, k] = mm(pack[g], wbuf[:, cols])
            if k:
                start(remote(xsend.at[c, k], xrecv.at[c, k - 1], xs.at[c, k - 1], xr.at[c, k - 1], at_x(k)))

    def place_of(packed_prow):
        spot = packed_prow.astype(I32)
        k = iota((1, NZ * CAP), 1) // CAP * PROWS + spot - 1
        k = jnp.where(spot > 0, k, -1)
        return jnp.where(iota((NZ * PROWS, NZ * CAP), 0) == k, 1.0, 0.0).astype(BF16)

    spread = []

    def take_packed(c):
        if not spread:
            spread.append(place_of(msend[x][0:1]))
            for k in (1, 2, 3):
                remote(msend.at[0], mrecv.at[k - 1], ms.at[k - 1], mr.at[k - 1], at_x(k)).wait_recv()
                spread.append(place_of(mrecv[k - 1][0:1]))
        total = mm(spread[0], xsend[c, 0].astype(BF16))
        for k in (1, 3, 2):
            remote(xsend.at[c, k], xrecv.at[c, k - 1], xs.at[c, k - 1], xr.at[c, k - 1], at_x(k)).wait_recv()
            total += mm(spread[k], xrecv[c, k - 1].astype(BF16))
        acc[c] = total

    def hops(direction, unit):
        return NZ // 2 if (unit + direction) % 2 == 0 else NZ // 2 - 1

    def ring_dest(direction, unit, step):
        left = hops(direction, unit) - step
        return lax.rem(z + (left if direction == 0 else -left) + NZ, NZ)

    def b_value(c, part, d):
        rows = pl.ds(pl.multiple_of(d * LANES + part * BROWS, BROWS), BROWS)
        return mm(sel[rows, :], wbuf[:, (NA + c) * LANES : (NA + c + 1) * LANES])

    def counts_of(d):
        return jnp.broadcast_to(cnt[pl.ds(d, 1), :], (8, LANES))

    def b_rows(u):
        return BROWS + 8 if u == 0 else BROWS

    def b_copy(direction, u, step):
        rows = pl.ds(0, b_rows(u))
        source = bown.at[direction, u, rows] if step == 0 else bring.at[direction, step - 1, u, rows]
        return remote(
            source,
            bring.at[direction, step, u, rows],
            bs.at[direction, step, u],
            br.at[direction, step, u],
            at_z(1 if direction == 0 else -1),
        )

    def b_step(step):
        for u in range(NB * RB):
            c, part = u // RB, u % RB
            for direction in (0, 1):
                if step >= hops(direction, u):
                    continue
                d = ring_dest(direction, u, step)
                value = b_value(c, part, d)
                if step == 0:
                    bown[direction, u, 0:BROWS] = value
                    if u == 0:
                        bown[direction, u, BROWS : BROWS + 8] = counts_of(d)
                else:
                    b_copy(direction, u, step - 1).wait_recv()
                    bring[direction, step - 1, u, 0:BROWS] += value
                    if u == 0:
                        bring[direction, step - 1, u, BROWS : BROWS + 8] += counts_of(d)
                start(b_copy(direction, u, step))

    def b_last():
        for u in range(NB * RB):
            c, part = u // RB, u % RB
            cols = slice(c * LANES, (c + 1) * LANES)
            value = b_value(c, part, z)
            number = counts_of(z)
            for direction in (0, 1):
                step = hops(direction, u) - 1
                b_copy(direction, u, step).wait_recv()
                value += bring[direction, step, u, 0:BROWS]
                if u == 0:
                    number += bring[direction, step, u, BROWS : BROWS + 8]
            for g in range(BROWS // PROWS):
                bsend[part * (BROWS // PROWS) + g, 0:PROWS, cols] = value[g * PROWS : (g + 1) * PROWS]
            if u == 0:
                for g in range(NX):
                    bsend[g, PROWS : PROWS + 8, 0:LANES] = number
                    for other in range(1, NB):
                        bsend[g, PROWS : PROWS + 8, other * LANES : (other + 1) * LANES] = number
        for k in (2, 1, 3):
            start(remote(bsend.at[lax.rem(x + k, NX)], brecv.at[k - 1], bxs.at[k - 1], bxr.at[k - 1], at_x(k)))

    def a_copy(direction, c, step):
        return remote(
            acc.at[c, pl.ds(pl.multiple_of(ring_dest(direction, c, 0) * PROWS, PROWS), PROWS)]
            if step == 0
            else aring.at[direction, step - 1, c],
            aring.at[direction, step, c],
            az.at[direction, step, c],
            ar.at[direction, step, c],
            at_z(1 if direction == 0 else -1),
        )

    def a_step(c, step):
        for direction in (0, 1):
            if step >= hops(direction, c):
                continue
            if step:
                d = ring_dest(direction, c, step)
                a_copy(direction, c, step - 1).wait_recv()
                aring[direction, step - 1, c] += acc[c, pl.ds(pl.multiple_of(d * PROWS, PROWS), PROWS), :]
            start(a_copy(direction, c, step))

    b_step(0)
    for c in range(NA):
        send_packed(c)
    for what, step in ORDER:
        if what == "b":
            b_step(step)
        elif what == "x":
            take_packed(step)
        elif what == "bx":
            b_last()
        else:
            a_step(int(what[1]), step)

    for k in (1, 3, 2):
        remote(bsend.at[0], brecv.at[k - 1], bxs.at[k - 1], bxr.at[k - 1], at_x(k)).wait_recv()
    total = bsend[x] + brecv[0] + brecv[1] + brecv[2]
    here = iota((PROWS, LANES), 1) == x * PROWS + iota((PROWS, LANES), 0)
    number = jnp.sum(jnp.where(here, jnp.broadcast_to(total[PROWS : PROWS + 1, 0:LANES], (PROWS, LANES)), 0.0), axis=1, keepdims=True)
    number = jnp.maximum(number, 1.0)
    out[:, NA * LANES :] = total[0:PROWS] / number
    for c in range(NA):
        value = acc[c, pl.ds(pl.multiple_of(z * PROWS, PROWS), PROWS), :]
        for direction in (0, 1):
            step = hops(direction, c) - 1
            a_copy(direction, c, step).wait_recv()
            value += aring[direction, step, c]
        out[:, c * LANES : (c + 1) * LANES] = value / number

    for copy in halo + meta + started:
        copy.wait_send()


def on_device(exposure, psf_taps, col_warp, row_warp, row_patch, row_prow, owner_map):
    vmem = pl.BlockSpec(memory_space=pltpu.VMEM)
    anywhere = pl.BlockSpec(memory_space=pl.ANY)
    steps = NZ // 2
    dma = pltpu.SemaphoreType.DMA
    return pl.pallas_call(
        kernel,
        out_shape=jax.ShapeDtypeStruct((PROWS, W), F32),
        in_specs=[anywhere, vmem, anywhere, anywhere, vmem, vmem, vmem],
        out_specs=vmem,
        scratch_shapes=[
            pltpu.VMEM((R, W), F32),
            pltpu.VMEM((W, W), BF16),
            pltpu.VMEM((RO, R), BF16),
            pltpu.VMEM((W, W), BF16),
            pltpu.VMEM((R, W), BF16),
            pltpu.VMEM((RO, W), BF16),
            pltpu.VMEM((NX * NZ * PROWS, RO), BF16),
            pltpu.VMEM((NX, NZ * CAP, RO), BF16),
            pltpu.VMEM((2, 8, W), F32),
            pltpu.VMEM((2, 8, W), F32),
            pltpu.VMEM((NZ, LANES), F32),
            pltpu.VMEM((2, NB * RB, BROWS + 8, LANES), F32),
            pltpu.VMEM((2, steps, NB * RB, BROWS + 8, LANES), F32),
            pltpu.VMEM((NX, PROWS + 8, NB * LANES), F32),
            pltpu.VMEM((NX - 1, PROWS + 8, NB * LANES), F32),
            pltpu.VMEM((NA, NX, NZ * CAP, LANES), F32),
            pltpu.VMEM((NA, NX - 1, NZ * CAP, LANES), F32),
            pltpu.VMEM((NX, 8, NZ * CAP), F32),
            pltpu.VMEM((NX - 1, 8, NZ * CAP), F32),
            pltpu.VMEM((NA, NZ * PROWS, LANES), F32),
            pltpu.VMEM((2, steps, NA, PROWS, LANES), F32),
            dma((6,)),
            dma((2,)),
            dma((2,)),
            dma((2, steps, NB * RB)),
            dma((2, steps, NB * RB)),
            dma((NX - 1,)),
            dma((NX - 1,)),
            dma((NA, NX - 1)),
            dma((NA, NX - 1)),
            dma((NX - 1,)),
            dma((NX - 1,)),
            dma((2, steps, NA)),
            dma((2, steps, NA)),
        ],
        compiler_params=pltpu.CompilerParams(collective_id=0, has_side_effects=True),
    )(
        exposure,
        psf_taps,
        col_warp,
        row_warp,
        row_patch.reshape(1, RO),
        row_prow.reshape(1, RO),
        owner_map.reshape(1, -1),
    )


def solution(mesh):
    placed = (
        P(("band", "exp"), None),
        P(("band", "exp"), None),
        P(("band", "exp"), None),
        P(("band", "exp"), None),
        P(("band", "exp"), None),
        P(("band", "exp")),
        P("band"),
    )
    return jax.shard_map(
        on_device, mesh=mesh, in_specs=placed, out_specs=P(("band", "exp"), None), check_vma=False
    )
```

time: 748 us -> 66.5 us (0.09)
  waiting for transfers between devices: 536 us -> 0 us
  blocking collectives: 144 us -> 0 us
  Pallas kernels: 0 us -> 64.9 us
  starting transfers between devices: 15.5 us -> 0 us
  matrix products: 15.4 us -> 0 us
  between operations: 14.1 us -> 0.01 us
  other arithmetic: 13.8 us -> 0 us
  local copies, waits for them, and re-layouts: 9.05 us -> 1.47 us
    reduce_scatter x1 -> x0, waiting for transfers between devices: 536 us -> none  [on_device(): lax.psum_scatter(jax.ops.segment_sum(warped, local, num_segments=count +...]
    unnamed x1 -> x0, blocking collectives: 144 us -> none
    pallas_call x0 -> x1, Pallas kernels: none -> 64.9 us  [on_device(): pl.pallas_call(kernel, out_shape=jax.ShapeDtypeStruct((PROWS, W), F32), i...]
    ppermute x2 -> x0, starting transfers between devices: 15.5 us -> none  [the longest x1 11.7 us: extended(): lax.ppermute(lax.slice_in_dim(block, 0, width, axis=dim), axis, backward)]
    dot_general x2 -> x0, matrix products: 15.4 us -> none  [the longest x1 13.4 us: on_device(): jnp.dot(matched, col_warp, preferred_element_type=jnp.float32)]
    scatter-add x2 -> x0, other arithmetic: 9 us -> none  [the longest x1 5.75 us: on_device(): jax.ops.segment_sum(warped, local, num_segments=count + 1)[:count]]
  transfers between devices with their start and end apart: 3 -> 0, of which waited for: 1 -> 0; matrix products, arithmetic and copies ran while one was open for 1% -> 0% of each run, Pallas kernels for 0% -> 0%
where the time goes in v1:
time: 66.5 us; the launch traced here: 66.3 us
  Pallas kernels  64.9 us (98%)
  local copies, waits for them, and re-layouts  1.47 us (2%)
    pallas_call x1, Pallas kernels, on_device(): pl.pallas_call(kernel, out_shape=jax.ShapeDtypeStruct((PROWS, W), F32), i...  64.9 us
    unnamed x1, local copies, waits for them, and re-layouts  1.47 us

profile of v1, /device:TPU:24, one launch (start us, length us, event | category | flops | bytes accessed | tf_op | source)
XLA Modules:
  0.0 66.3 jit_solution(103739191706978310)
XLA Ops:
  0.0 64.9 %shard_map.73 = f32[32,512]{1,0:T(8,128)} custom-call(f32[1024,512]{1,0:T(8,128)} %expo.1, bf16[1,15]{1,0:T(2,128)(2,1)} %taps.1, bf16[512,512]{1,0:T(8,128)(2,1)} %cw_hbm.1, bf16[512,1024]{1,0:T(8,128)(2,1)} %rw_hbm.1, s32[1,512]{1,0:T(1,128)} %bitcast.3, s32[1,512]{1,0:T(1,128)} %bitcast.4, s32[1,64]{1,0:T(1,128)} %bitcast.5), custom_call_target="tpu_custom_call" | custom-call | tf_op jit(solution)/shard_map/pallas_call | solution.py:338
  64.9 1.5 %copy.9 = f32[32,512]{1,0:T(8,128)} copy(f32[32,512]{1,0:T(8,128)} %shard_map.73) | data formatting | bytes 131072

commit v2 on v0

v2 whole, which is shorter than its diff:
```python
import functools

import jax
import jax.numpy as jnp
from jax import lax
from jax.experimental import pallas as pl
from jax.experimental.pallas import tpu as pltpu
from jax.sharding import PartitionSpec as P

F32, BF16, I32 = jnp.float32, jnp.bfloat16, jnp.int32
MESH = pl.DeviceIdType.MESH

STRIP = 16
TAPS = 15
PROWS = 32
CAP = 16
NX, NZ = 4, 16
W, R, RO = 512, 1024, 512
LANES = 128

NC = W // LANES
OWN, OPP = 0, 1
NM = NZ - 1
SIDES = (1, 3)

UNITS = (
    (OWN, 0, 256, 40),
    (OWN, 256, 256, 32),
    (OPP, 0, 128, 40),
    (OPP, 128, 128, 32),
    (OPP, 256, 128, 32),
    (OPP, 384, 128, 32),
)
NOWN = sum(u[0] == OWN for u in UNITS)
GROUPS = ((0, 2), (2, 4), (4, 8), (8, 12), (12, 16))
ORDER = (
    (2, 0, 1), (2, 1, 1), (3, 1, 1), (3, 0, 1), ("x", 0), (4, 0, 1), (4, 1, 1), (0, 0, 0), (5, 1, 1), (5, 0, 1),
    (1, 1, 0), (0, 1, 0), ("x", 1), (2, 0, 2), (2, 1, 2), (1, 0, 0), (3, 0, 2), (3, 1, 2), (4, 0, 2), (4, 1, 2),
    (5, 1, 2), (0, 0, 1), (1, 1, 1), (5, 0, 2), (2, 0, 3), ("x", 2), (0, 1, 1), (1, 0, 1), (2, 1, 3), (3, 0, 3),
    (3, 1, 3), (4, 0, 3), (4, 1, 3), (5, 1, 3), (0, 0, 2), (1, 1, 2), (5, 0, 3), ("x", 3), (2, 0, 4), (0, 1, 2),
    (1, 0, 2), (2, 1, 4), (3, 0, 4), (3, 1, 4), (4, 0, 4), (4, 1, 4), (5, 1, 4), (0, 0, 3), (1, 1, 3), (5, 0, 4),
    ("x", 4), (2, 0, 5), (0, 1, 3), (1, 0, 3), (2, 1, 5), (3, 0, 5), (3, 1, 5), (4, 0, 5), (4, 1, 5), (5, 1, 5),
    (0, 0, 4), (1, 1, 4), (5, 0, 5), (2, 0, 6), (0, 1, 4), (1, 0, 4), (2, 1, 6), (3, 0, 6), (3, 1, 6), (4, 0, 6),
    (4, 1, 6), (5, 1, 6), (0, 0, 5), (1, 1, 5), (5, 0, 6), (2, 0, 7), (0, 1, 5), (1, 0, 5), (3, 1, 7), (4, 0, 7),
    (5, 1, 7), (0, 0, 6), (1, 1, 6), ("o", 2), (0, 1, 6), ("o", 3), (1, 0, 6), ("o", 5), ("o", 4), (0, 0, 7),
    (1, 1, 7),
)


def far(n, direction):
    return NZ // 2 if (n + direction) % 2 == 0 else NZ // 2 - 1


def spot_of(n, direction, step):
    left = far(n, direction) - step
    away = left if direction == 0 else NZ - left
    return 2 * (NZ // 2 - away) if away <= NZ // 2 else 2 * (away - NZ // 2 - 1) + 1


def nt(a, b):
    return lax.dot_general(a, b, (((1,), (1,)), ((), ())), preferred_element_type=F32)


def mm(a, b):
    return jnp.dot(a, b, preferred_element_type=F32)


def iota(shape, dim):
    return lax.broadcasted_iota(I32, shape, dim)


def equal(a, b):
    return jnp.where(a == b, 1.0, 0.0).astype(BF16)


def kernel(
    expo, taps_hbm, cw_hbm, rw_hbm, patch_hbm, prow_hbm, owner_hbm, out,
    ex, strips, taps, cw, rw, patch, prow, owner, mat, corr, ybuf, wbuf, sel, pack, halo_out, halo_in,
    msend, mrecv, in_sem, hs, hr, ms, mr, xs, xr, rs, rr, os, oR, *buffers,
):
    buffers = list(buffers)

    def take(number):
        return [buffers.pop(0) for _ in range(number)]

    count = len(UNITS)
    acc, ring, osend, orecv = take(count), take(count), take(count - NOWN), take(count - NOWN)
    xsend, xrecv, place = take(len(GROUPS)), take(len(GROUPS)), take(len(GROUPS))
    e = lax.axis_index("exp")
    x, z = e // NZ, lax.rem(e, NZ)

    def dev(i):
        return {"exp": i}

    def at_z(d):
        return x * NZ + lax.rem(z + d + NZ, NZ)

    def at_x(d):
        return lax.rem(x + d + NX, NX) * NZ + z

    def remote(src, dst, s, r, target):
        return pltpu.make_async_remote_copy(
            src_ref=src, dst_ref=dst, send_sem=s, recv_sem=r, device_id=dev(target), device_id_type=MESH
        )

    nxt, prv = lax.rem(e + 1, NX * NZ), lax.rem(e + NX * NZ - 1, NX * NZ)

    loads = []

    def load(src, dst):
        copy = pltpu.make_async_copy(src, dst, in_sem.at[len(loads)])
        copy.start()
        loads.append(copy)
        return copy

    strip_loads = [load(expo.at[pl.ds(0, STRIP)], strips.at[0]), load(expo.at[pl.ds(R - STRIP, STRIP)], strips.at[1])]
    barrier = pltpu.get_barrier_semaphore()
    peers = [nxt, prv, at_z(1), at_z(-1), at_x(1), at_x(3), at_x(2)]
    for peer in peers:
        pl.semaphore_signal(barrier, inc=1, device_id=dev(peer), device_id_type=MESH)
    key_loads = [load(owner_hbm, owner), load(patch_hbm, patch), load(prow_hbm, prow)]
    piece_load = load(expo, ex)
    row_load = load(rw_hbm, rw)
    mat_loads = [load(taps_hbm, taps), load(cw_hbm, cw)]

    for copy in strip_loads:
        copy.wait()

    def means(strip):
        total = jnp.sum(strip, axis=0, keepdims=True)
        parts = [
            jnp.broadcast_to(
                jnp.sum(total[:, b * LANES : (b + 1) * LANES], axis=1, keepdims=True) * (1.0 / (STRIP * LANES)), (1, LANES)
            )
            for b in range(NC)
        ]
        return jnp.concatenate(parts, axis=1)

    first, last = means(strips[0]), means(strips[1])
    halo_out[0] = jnp.broadcast_to(first, (8, W))
    halo_out[1] = jnp.broadcast_to(last, (8, W))
    pl.semaphore_wait(barrier, len(peers))
    halo = [
        remote(halo_out.at[0], halo_in.at[0], hs, hr.at[0], prv),
        remote(halo_out.at[1], halo_in.at[1], hs, hr.at[1], nxt),
    ]
    for copy in halo:
        copy.start()

    for copy in key_loads:
        copy.wait()
    eye = iota((NX * NZ, NX * NZ), 0) == iota((NX * NZ, NX * NZ), 1)
    owner_col = jnp.sum(jnp.where(eye, jnp.broadcast_to(owner[...], eye.shape), 0), axis=1, keepdims=True)
    own_of = owner_col == patch[...]
    dest = jnp.sum(jnp.where(own_of, iota((NX * NZ, RO), 0), 0), axis=0, keepdims=True)
    dest_x, dest_z = dest // NZ, lax.rem(dest, NZ)
    one_hot = jnp.where(own_of, 1.0, 0.0)
    before = jnp.where(iota((RO, RO), 0) < iota((RO, RO), 1), 1.0, 0.0).astype(BF16)
    earlier = mm(one_hot.astype(BF16), before)
    rank = jnp.sum(one_hot * earlier, axis=0, keepdims=True).astype(I32)
    away = lax.rem(dest_z - z + NZ, NZ)
    near = NZ // 2
    spot = jnp.where(away == 0, NZ - 1, jnp.where(away <= near, 2 * (near - away), 2 * (away - near) - 1))
    slot = spot * CAP + rank

    prow_row = jnp.broadcast_to((prow[...] + 1).astype(F32), (8, RO)).astype(BF16)
    meta = []
    for i, k in enumerate(SIDES):
        to = dest_x == lax.rem(x + k, NX)
        pack[i] = equal(iota((NZ * CAP, RO), 0), jnp.where(to, slot, -1))
        msend[i] = nt(prow_row, pack[i])
        meta.append(remote(msend.at[i], mrecv.at[i], ms, mr.at[i], at_x(k)))
        meta[-1].start()

    oz = equal(iota((NZ, RO), 0), spot)
    counts = []
    for kind in (OWN, OPP):
        to = dest_x == lax.rem(x + 2 * kind, NX)
        key = jnp.where(to, spot * PROWS + prow[...], -1)
        sel[kind] = equal(iota((NZ * PROWS, RO), 0), key)
        counts.append(nt(oz, equal(iota((LANES, RO), 0), jnp.where(to, prow[...], -1))))

    offset = iota((LANES, 3 * LANES), 0) - iota((LANES, 3 * LANES), 1) + (LANES + (TAPS - 1) // 2)
    for copy in mat_loads:
        copy.wait()
    band = jnp.zeros((LANES, 3 * LANES), F32)
    tap = taps[...].astype(F32)
    for t in range(TAPS):
        band = jnp.where(offset == t, jnp.broadcast_to(tap[:, t : t + 1], (LANES, 3 * LANES)), band)
    band = band.astype(BF16)
    for b in range(NC):
        low, high = max(b - 1, 0), min(b + 2, NC)
        strip = band[:, (low - b + 1) * LANES : (high - b + 1) * LANES]
        mat[b * LANES : (b + 1) * LANES, :] = mm(strip, cw[low * LANES : high * LANES, :]).astype(BF16)

    piece_load.wait()
    row_load.wait()
    for copy in halo:
        copy.wait_recv()
    off_next = last - halo_in[0][0:1]
    off_prev = halo_in[1][0:1] - first
    shift = -0.5 * off_next + 0.5 * off_prev

    def x_copy(g, i):
        return remote(xsend[g].at[i], xrecv[g].at[i], xs.at[g], xr.at[g, i], at_x(SIDES[i]))

    def chain_copy(n, direction, step):
        m = step if direction == 0 else far(n, 0) + step
        source = ring[n].at[m - 1] if step else acc[n].at[spot_of(n, direction, 0)]
        return remote(source, ring[n].at[m], rs.at[n], rr.at[n, m], at_z(1 if direction == 0 else -1))

    def chain_step(n, direction, step):
        if step:
            m = step if direction == 0 else far(n, 0) + step
            chain_copy(n, direction, step - 1).wait_recv()
            ring[n][m - 1] += acc[n][spot_of(n, direction, step)]
        chain_copy(n, direction, step).start()

    def chain_total(n):
        total = acc[n][NZ - 1]
        for direction in (0, 1):
            step = far(n, direction) - 1
            chain_copy(n, direction, step).wait_recv()
            total += ring[n][step if direction == 0 else far(n, 0) + step]
        return total

    def opp_copy(n):
        return remote(osend[n - NOWN], orecv[n - NOWN], os.at[n - NOWN], oR.at[n - NOWN], at_x(2))

    def opp_last(n):
        osend[n - NOWN][...] = chain_total(n)
        opp_copy(n).start()

    def spread(packed, i):
        at = packed[0:1].astype(I32)
        lane = iota((1, NZ * CAP), 1) // CAP
        key = jnp.where(at > 0, lane * PROWS + at - 1, -1)
        for g, (low, high) in enumerate(GROUPS):
            part = key[:, low * CAP : high * CAP]
            place[g][i] = equal(iota(((high - low) * PROWS, (high - low) * CAP), 0) + low * PROWS, part)
        return nt(equal(iota((NZ, NZ * CAP), 0), lane), equal(iota((LANES, NZ * CAP), 0), at - 1))

    def columns(n):
        return slice(UNITS[n][1], UNITS[n][1] + UNITS[n][2])

    def take_packed(g):
        low, high = GROUPS[g]
        for i in (0, 1):
            x_copy(g, i).wait_recv()
        for n in range(NOWN):
            shape = (high - low, PROWS, UNITS[n][2])
            total = acc[n][low:high, 0:PROWS].reshape(shape[0] * PROWS, shape[2])
            for i in (0, 1):
                total += mm(place[g][i], xrecv[g][i, :, columns(n)].astype(BF16))
            acc[n][low:high, 0:PROWS] = total.reshape(shape)

    def fill_counts(n, number):
        tile = jnp.broadcast_to(number[:, None, :], (NZ, 8, LANES))
        for part in range(UNITS[n][2] // LANES):
            acc[n][:, PROWS:, part * LANES : (part + 1) * LANES] = tile

    def send_packed(g):
        low, high = GROUPS[g]
        for i in (0, 1):
            xsend[g][i] = mm(pack[i, low * CAP : high * CAP], wbuf[...])
            x_copy(g, i).start()

    def dense(n):
        acc[n][:, 0:PROWS] = mm(sel[UNITS[n][0]], wbuf[:, columns(n)]).reshape(NZ, PROWS, UNITS[n][2])

    fill_counts(NOWN, counts[OPP])

    corr[...] = (ex[...] + shift).astype(BF16)
    ybuf[...] = mm(rw[...], corr[...]).astype(BF16)
    wbuf[...] = mm(ybuf[...], mat[...]).astype(BF16)
    send_packed(0)
    for n in range(NOWN, count):
        dense(n)
        for direction in (0, 1):
            chain_step(n, direction, 0)
    for g in range(1, len(GROUPS)):
        send_packed(g)
    for n in range(NOWN):
        dense(n)

    number = counts[OWN]
    for i in (0, 1):
        meta[i].wait_recv()
        number += spread(mrecv[i], i)
    fill_counts(0, number)

    for step in ORDER:
        if step[0] == "x":
            take_packed(step[1])
        elif step[0] == "o":
            opp_last(step[1])
        else:
            chain_step(*step)

    diag = iota((PROWS, LANES), 1) == iota((PROWS, LANES), 0)
    for n in range(NOWN, count):
        opp_copy(n).wait_recv()
    for n in range(NOWN):
        total = chain_total(n)
        if n == 0:
            number = jnp.broadcast_to(total[PROWS : PROWS + 1, 0:LANES] + orecv[0][PROWS : PROWS + 1, 0:LANES], (PROWS, LANES))
            number = jnp.maximum(jnp.sum(jnp.where(diag, number, 0.0), axis=1, keepdims=True), 1.0)
        for c in range(UNITS[n][2] // LANES):
            first_column = UNITS[n][1] + c * LANES
            o = next(o for o in range(NOWN, count) if UNITS[o][1] <= first_column < UNITS[o][1] + UNITS[o][2])
            other = orecv[o - NOWN][0:PROWS, first_column - UNITS[o][1] : first_column - UNITS[o][1] + LANES]
            out[:, first_column : first_column + LANES] = (total[0:PROWS, c * LANES : (c + 1) * LANES] + other) / number

    remote(halo_out, halo_in, hs, hr.at[0], prv).wait_send()
    remote(msend, mrecv, ms, mr.at[0], at_x(1)).wait_send()
    for g in range(len(GROUPS)):
        remote(xsend[g], xrecv[g], xs.at[g], xr.at[g, 0], at_x(1)).wait_send()
    for n in range(count):
        remote(ring[n], ring[n], rs.at[n], rr.at[n, 0], at_z(1)).wait_send()
    for n in range(NOWN, count):
        opp_copy(n).wait_send()


def on_device(exposure, psf_taps, col_warp, row_warp, row_patch, row_prow, owner_map):
    anywhere = pl.BlockSpec(memory_space=pl.ANY)
    dma = pltpu.SemaphoreType.DMA
    vmem = pltpu.VMEM
    blocks = [(rows, width) for _, _, width, rows in UNITS]
    packs = [vmem((2, (high - low) * CAP, W), F32) for low, high in GROUPS]
    places = [vmem((2, (high - low) * PROWS, (high - low) * CAP), BF16) for low, high in GROUPS]
    others = [vmem(block, F32) for block in blocks[NOWN:]]
    return pl.pallas_call(
        kernel,
        out_shape=vmem((PROWS, W), F32),
        in_specs=[anywhere] * 7,
        out_specs=pl.BlockSpec(memory_space=vmem),
        scratch_shapes=[
            vmem((R, W), F32),
            vmem((2, STRIP, W), F32),
            vmem((1, TAPS), BF16),
            vmem((W, W), BF16),
            vmem((RO, R), BF16),
            vmem((1, RO), I32),
            vmem((1, RO), I32),
            vmem((1, NX * NZ), I32),
            vmem((W, W), BF16),
            vmem((R, W), BF16),
            vmem((RO, W), BF16),
            vmem((RO, W), BF16),
            vmem((2, NZ * PROWS, RO), BF16),
            vmem((2, NZ * CAP, RO), BF16),
            vmem((2, 8, W), F32),
            vmem((2, 8, W), F32),
            vmem((2, 8, NZ * CAP), F32),
            vmem((2, 8, NZ * CAP), F32),
            dma((9,)),
            dma(()),
            dma((2,)),
            dma(()),
            dma((2,)),
            dma((len(GROUPS),)),
            dma((len(GROUPS), 2)),
            dma((len(UNITS),)),
            dma((len(UNITS), NM)),
            dma((len(UNITS) - NOWN,)),
            dma((len(UNITS) - NOWN,)),
        ]
        + [vmem((NZ, *block), F32) for block in blocks]
        + [vmem((NM, *block), F32) for block in blocks]
        + others
        + others
        + packs
        + packs
        + places,
        compiler_params=pltpu.CompilerParams(collective_id=0, has_side_effects=True),
    )(
        exposure,
        psf_taps,
        col_warp,
        row_warp,
        row_patch.reshape(1, RO),
        row_prow.reshape(1, RO),
        owner_map.reshape(1, -1),
    )


def solution(mesh):
    placed = (
        P(("band", "exp"), None),
        P(("band", "exp"), None),
        P(("band", "exp"), None),
        P(("band", "exp"), None),
        P(("band", "exp"), None),
        P(("band", "exp")),
        P("band"),
    )
    return jax.shard_map(
        on_device, mesh=mesh, in_specs=placed, out_specs=P(("band", "exp"), None), check_vma=False
    )
```

time: 748 us -> 52.5 us (0.07)
  waiting for transfers between devices: 536 us -> 0 us
  blocking collectives: 144 us -> 0 us
  Pallas kernels: 0 us -> 51.7 us
  starting transfers between devices: 15.5 us -> 0 us
  matrix products: 15.4 us -> 0 us
  between operations: 14.1 us -> 0.01 us
  other arithmetic: 13.8 us -> 0 us
  local copies, waits for them, and re-layouts: 9.05 us -> 0.63 us
    reduce_scatter x1 -> x0, waiting for transfers between devices: 536 us -> none  [on_device(): lax.psum_scatter(jax.ops.segment_sum(warped, local, num_segments=count +...]
    unnamed x1 -> x0, blocking collectives: 144 us -> none
    pallas_call x0 -> x1, Pallas kernels: none -> 51.7 us  [on_device(): pl.pallas_call(kernel, out_shape=vmem((PROWS, W), F32), in_specs=[anywher...]
    ppermute x2 -> x0, starting transfers between devices: 15.5 us -> none  [the longest x1 11.7 us: extended(): lax.ppermute(lax.slice_in_dim(block, 0, width, axis=dim), axis, backward)]
    dot_general x2 -> x0, matrix products: 15.4 us -> none  [the longest x1 13.4 us: on_device(): jnp.dot(matched, col_warp, preferred_element_type=jnp.float32)]
    scatter-add x2 -> x0, other arithmetic: 9 us -> none  [the longest x1 5.75 us: on_device(): jax.ops.segment_sum(warped, local, num_segments=count + 1)[:count]]
  transfers between devices with their start and end apart: 3 -> 0, of which waited for: 1 -> 0; matrix products, arithmetic and copies ran while one was open for 1% -> 0% of each run, Pallas kernels for 0% -> 0%
where the time goes in v2:
time: 52.5 us; the launch traced here: 52.4 us
  Pallas kernels  51.7 us (98%)
  local copies, waits for them, and re-layouts  0.63 us (1%)
    pallas_call x1, Pallas kernels, on_device(): pl.pallas_call(kernel, out_shape=vmem((PROWS, W), F32), in_specs=[anywher...  51.7 us

profile of v2, /device:TPU:24, one launch (start us, length us, event | category | flops | bytes accessed | tf_op | source)
XLA Modules:
  0.0 52.4 jit_solution(2222964924224795423)
XLA Ops:
  0.0 51.7 %shard_map.73 = f32[32,512]{1,0:T(8,128)S(1)} custom-call(f32[1024,512]{1,0:T(8,128)} %expo.1, bf16[1,15]{1,0:T(2,128)(2,1)} %taps_hbm.1, bf16[512,512]{1,0:T(8,128)(2,1)} %cw_hbm.1, bf16[512,1024]{1,0:T(8,128)(2,1)} %rw_hbm.1, s32[1,512]{1,0:T(1,128)} %bitcast.3, s32[1,512]{1,0:T(1,128)} %bitcast.4, s32[1,64]{1,0:T(1,128)} %bitcast.5), custom_call_target="tpu_custom_call" | custom-call | tf_op jit(solution)/shard_map/pallas_call | solution.py:332
  51.7 0.6 %copy.9 = f32[32,512]{1,0:T(8,128)} copy(f32[32,512]{1,0:T(8,128)S(1)} %shard_map.73) | data formatting | bytes 131072

commit v3 on v2

--- a/solution.py
+++ b/solution.py
@@ -21,40 +21,49 @@
 NC = W // LANES
 OWN, OPP = 0, 1
 NM = NZ - 1
-SIDES = (1, 3)
+SIDES = (1, 3, 2)
 
 UNITS = (
-    (OWN, 0, 256, 40),
-    (OWN, 256, 256, 32),
-    (OPP, 0, 128, 40),
+    (OWN, 0, 128, 33),
+    (OWN, 128, 128, 32),
+    (OWN, 256, 128, 32),
+    (OWN, 384, 128, 32),
+    (OPP, 0, 128, 33),
     (OPP, 128, 128, 32),
-    (OPP, 256, 128, 32),
-    (OPP, 384, 128, 32),
 )
 NOWN = sum(u[0] == OWN for u in UNITS)
-GROUPS = ((0, 2), (2, 4), (4, 8), (8, 12), (12, 16))
+ZFIRST = 256
+NEAR = (2, 2)
+SPOT = (15, 13, 11, 9, 7, 5, 3, 1, 0, 2, 4, 6, 8, 10, 12, 14)
+GROUPS = ((0, 2), (2, 4), (4, 6), (6, 8), (8, 10), (10, 12), (12, 14), (14, 16))
 ORDER = (
-    (2, 0, 1), (2, 1, 1), (3, 1, 1), (3, 0, 1), ("x", 0), (4, 0, 1), (4, 1, 1), (0, 0, 0), (5, 1, 1), (5, 0, 1),
-    (1, 1, 0), (0, 1, 0), ("x", 1), (2, 0, 2), (2, 1, 2), (1, 0, 0), (3, 0, 2), (3, 1, 2), (4, 0, 2), (4, 1, 2),
-    (5, 1, 2), (0, 0, 1), (1, 1, 1), (5, 0, 2), (2, 0, 3), ("x", 2), (0, 1, 1), (1, 0, 1), (2, 1, 3), (3, 0, 3),
-    (3, 1, 3), (4, 0, 3), (4, 1, 3), (5, 1, 3), (0, 0, 2), (1, 1, 2), (5, 0, 3), ("x", 3), (2, 0, 4), (0, 1, 2),
-    (1, 0, 2), (2, 1, 4), (3, 0, 4), (3, 1, 4), (4, 0, 4), (4, 1, 4), (5, 1, 4), (0, 0, 3), (1, 1, 3), (5, 0, 4),
-    ("x", 4), (2, 0, 5), (0, 1, 3), (1, 0, 3), (2, 1, 5), (3, 0, 5), (3, 1, 5), (4, 0, 5), (4, 1, 5), (5, 1, 5),
-    (0, 0, 4), (1, 1, 4), (5, 0, 5), (2, 0, 6), (0, 1, 4), (1, 0, 4), (2, 1, 6), (3, 0, 6), (3, 1, 6), (4, 0, 6),
-    (4, 1, 6), (5, 1, 6), (0, 0, 5), (1, 1, 5), (5, 0, 6), (2, 0, 7), (0, 1, 5), (1, 0, 5), (3, 1, 7), (4, 0, 7),
-    (5, 1, 7), (0, 0, 6), (1, 1, 6), ("o", 2), (0, 1, 6), ("o", 3), (1, 0, 6), ("o", 5), ("o", 4), (0, 0, 7),
-    (1, 1, 7),
+    (4, 0, 1), (4, 2, 1), (4, 1, 1), (4, 3, 1), (5, 2, 1), (5, 0, 1), (5, 1, 1), (5, 3, 1), ("x", 0), (0, 0, 0),
+    (1, 2, 0), (2, 0, 0), (3, 2, 0), (1, 0, 0), (3, 0, 0), (4, 0, 2), (4, 2, 2), ("x", 1), (0, 2, 0), (2, 2, 0),
+    (5, 0, 2), (5, 2, 2), (1, 2, 1), (0, 0, 1), (3, 2, 1), (2, 0, 1), (1, 0, 1), ("x", 2), (3, 0, 1), (4, 0, 3),
+    (4, 2, 3), (0, 2, 1), (5, 0, 3), (2, 2, 1), (5, 2, 3), ("x", 3), (1, 2, 2), (0, 0, 2), (3, 2, 2), (2, 0, 2),
+    (1, 0, 2), (3, 0, 2), (4, 0, 4), (4, 2, 4), ("x", 4), (0, 2, 2), (5, 0, 4), (2, 2, 2), (5, 2, 4), (1, 2, 3),
+    (0, 0, 3), (3, 2, 3), (2, 0, 3), (1, 0, 3), ("x", 5), (0, 1, 0), (1, 1, 0), (2, 1, 0), (3, 1, 0), (3, 0, 3),
+    (4, 0, 5), (0, 2, 3), (2, 2, 3), ("x", 6), (0, 3, 0), (1, 3, 0), (2, 3, 0), (3, 3, 0), (0, 0, 4), (5, 2, 5),
+    (2, 0, 4), (1, 2, 4), (1, 0, 4), (3, 2, 4), (0, 1, 1), (1, 1, 1), (2, 1, 1), ("x", 7), (3, 1, 1), (3, 0, 4),
+    (0, 2, 4), (2, 2, 4), (0, 3, 1), (1, 3, 1), (0, 0, 5), (2, 3, 1), (2, 0, 5), (3, 3, 1), ("o", 4), (1, 2, 5),
+    (3, 2, 5), ("o", 5),
 )
 
 
-def far(n, direction):
-    return NZ // 2 if (n + direction) % 2 == 0 else NZ // 2 - 1
-
-
-def spot_of(n, direction, step):
-    left = far(n, direction) - step
-    away = left if direction == 0 else NZ - left
-    return 2 * (NZ // 2 - away) if away <= NZ // 2 else 2 * (away - NZ // 2 - 1) + 1
+def chains(n):
+    out, m, near = [], 0, NEAR[UNITS[n][0]]
+    for direction in (0, 1):
+        far = NZ // 2 if (n + direction) % 2 == 0 else NZ // 2 - 1
+        for top, bottom in ((far, near), (near, 0)) if near else ((far, 0),):
+            left = (*range(top, bottom, -1), 0)
+            out.append((direction, left, m))
+            m += len(left) - 1
+    return out
+
+
+def spot_of(chain, step):
+    direction, left, _ = chain
+    return SPOT[left[step] if direction == 0 else NZ - left[step]]
 
 
 def nt(a, b):
@@ -76,7 +85,7 @@
 def kernel(
     expo, taps_hbm, cw_hbm, rw_hbm, patch_hbm, prow_hbm, owner_hbm, out,
     ex, strips, taps, cw, rw, patch, prow, owner, mat, corr, ybuf, wbuf, sel, pack, halo_out, halo_in,
-    msend, mrecv, in_sem, hs, hr, ms, mr, xs, xr, rs, rr, os, oR, *buffers,
+    msend, mrecv, in_sem, hs, hr, ms, mr, xs, ys, xr, rs, rr, os, oR, *buffers,
 ):
     buffers = list(buffers)
 
@@ -86,6 +95,7 @@
     count = len(UNITS)
     acc, ring, osend, orecv = take(count), take(count), take(count - NOWN), take(count - NOWN)
     xsend, xrecv, place = take(len(GROUPS)), take(len(GROUPS)), take(len(GROUPS))
+    ysend, yrecv = take(len(GROUPS)), take(len(GROUPS))
     e = lax.axis_index("exp")
     x, z = e // NZ, lax.rem(e, NZ)
 
@@ -116,6 +126,8 @@
     strip_loads = [load(expo.at[pl.ds(0, STRIP)], strips.at[0]), load(expo.at[pl.ds(R - STRIP, STRIP)], strips.at[1])]
     barrier = pltpu.get_barrier_semaphore()
     peers = [nxt, prv, at_z(1), at_z(-1), at_x(1), at_x(3), at_x(2)]
+    for hop in sorted({near + 1 for near in NEAR if near}):
+        peers += [at_z(hop), at_z(-hop)]
     for peer in peers:
         pl.semaphore_signal(barrier, inc=1, device_id=dev(peer), device_id_type=MESH)
     key_loads = [load(owner_hbm, owner), load(patch_hbm, patch), load(prow_hbm, prow)]
@@ -159,8 +171,7 @@
     earlier = mm(one_hot.astype(BF16), before)
     rank = jnp.sum(one_hot * earlier, axis=0, keepdims=True).astype(I32)
     away = lax.rem(dest_z - z + NZ, NZ)
-    near = NZ // 2
-    spot = jnp.where(away == 0, NZ - 1, jnp.where(away <= near, 2 * (near - away), 2 * (away - near) - 1))
+    spot = sum(jnp.where(away == i, SPOT[i], 0) for i in range(NZ))
     slot = spot * CAP + rank
 
     prow_row = jnp.broadcast_to((prow[...] + 1).astype(F32), (8, RO)).astype(BF16)
@@ -202,33 +213,39 @@
     shift = -0.5 * off_next + 0.5 * off_prev
 
     def x_copy(g, i):
-        return remote(xsend[g].at[i], xrecv[g].at[i], xs.at[g], xr.at[g, i], at_x(SIDES[i]))
-
-    def chain_copy(n, direction, step):
-        m = step if direction == 0 else far(n, 0) + step
-        source = ring[n].at[m - 1] if step else acc[n].at[spot_of(n, direction, 0)]
-        return remote(source, ring[n].at[m], rs.at[n], rr.at[n, m], at_z(1 if direction == 0 else -1))
-
-    def chain_step(n, direction, step):
+        source, target = (xsend[g].at[i], xrecv[g].at[i]) if i < 2 else (ysend[g], yrecv[g])
+        return remote(source, target, (xs if i < 2 else ys).at[g], xr.at[g, i], at_x(SIDES[i]))
+
+    def rows_of(n):
+        return pl.ds(0, UNITS[n][3])
+
+    def chain_copy(n, chain, step):
+        direction, left, m = chain
+        hop, rows = left[step] - left[step + 1], rows_of(n)
+        source = ring[n].at[m + step - 1, rows] if step else acc[n].at[spot_of(chain, 0), rows]
+        return remote(source, ring[n].at[m + step, rows], rs.at[n], rr.at[n, m + step], at_z(hop if direction == 0 else -hop))
+
+    def chain_step(n, c, step):
+        chain = chains(n)[c]
         if step:
-            m = step if direction == 0 else far(n, 0) + step
-            chain_copy(n, direction, step - 1).wait_recv()
-            ring[n][m - 1] += acc[n][spot_of(n, direction, step)]
-        chain_copy(n, direction, step).start()
+            chain_copy(n, chain, step - 1).wait_recv()
+            ring[n][chain[2] + step - 1, rows_of(n)] += acc[n][spot_of(chain, step), rows_of(n)]
+        chain_copy(n, chain, step).start()
 
     def chain_total(n):
-        total = acc[n][NZ - 1]
-        for direction in (0, 1):
-            step = far(n, direction) - 1
-            chain_copy(n, direction, step).wait_recv()
-            total += ring[n][step if direction == 0 else far(n, 0) + step]
+        total = acc[n][SPOT[0], rows_of(n)]
+        for chain in chains(n):
+            last = len(chain[1]) - 2
+            chain_copy(n, chain, last).wait_recv()
+            total += ring[n][chain[2] + last, rows_of(n)]
         return total
 
     def opp_copy(n):
-        return remote(osend[n - NOWN], orecv[n - NOWN], os.at[n - NOWN], oR.at[n - NOWN], at_x(2))
+        rows, o = rows_of(n), n - NOWN
+        return remote(osend[o].at[rows], orecv[o].at[rows], os.at[o], oR.at[o], at_x(2))
 
     def opp_last(n):
-        osend[n - NOWN][...] = chain_total(n)
+        osend[n - NOWN][rows_of(n), :] = chain_total(n)
         opp_copy(n).start()
 
     def spread(packed, i):
@@ -245,48 +262,59 @@
 
     def take_packed(g):
         low, high = GROUPS[g]
-        for i in (0, 1):
+        for i in (0, 1, 2):
             x_copy(g, i).wait_recv()
         for n in range(NOWN):
             shape = (high - low, PROWS, UNITS[n][2])
             total = acc[n][low:high, 0:PROWS].reshape(shape[0] * PROWS, shape[2])
             for i in (0, 1):
                 total += mm(place[g][i], xrecv[g][i, :, columns(n)].astype(BF16))
+            if UNITS[n][1] >= ZFIRST:
+                part = slice(UNITS[n][1] - ZFIRST, UNITS[n][1] - ZFIRST + UNITS[n][2])
+                total += mm(place[g][2], yrecv[g][:, part].astype(BF16))
             acc[n][low:high, 0:PROWS] = total.reshape(shape)
 
     def fill_counts(n, number):
-        tile = jnp.broadcast_to(number[:, None, :], (NZ, 8, LANES))
         for part in range(UNITS[n][2] // LANES):
-            acc[n][:, PROWS:, part * LANES : (part + 1) * LANES] = tile
-
-    def send_packed(g):
-        low, high = GROUPS[g]
-        for i in (0, 1):
-            xsend[g][i] = mm(pack[i, low * CAP : high * CAP], wbuf[...])
-            x_copy(g, i).start()
-
-    def dense(n):
-        acc[n][:, 0:PROWS] = mm(sel[UNITS[n][0]], wbuf[:, columns(n)]).reshape(NZ, PROWS, UNITS[n][2])
+            acc[n][:, PROWS : PROWS + 1, part * LANES : (part + 1) * LANES] = number[:, None, :]
+
+    def dense(kind, width):
+        total = mm(sel[kind], wbuf[:, 0:width])
+        for n in range(count):
+            if UNITS[n][0] == kind:
+                acc[n][:, 0:PROWS] = total[:, columns(n)].reshape(NZ, PROWS, UNITS[n][2])
 
     fill_counts(NOWN, counts[OPP])
 
     corr[...] = (ex[...] + shift).astype(BF16)
     ybuf[...] = mm(rw[...], corr[...]).astype(BF16)
     wbuf[...] = mm(ybuf[...], mat[...]).astype(BF16)
-    send_packed(0)
+    packed = [mm(pack[i], wbuf[...] if i < 2 else wbuf[:, ZFIRST:]) for i in (0, 1, 2)]
+    for g, (low, high) in enumerate(GROUPS):
+        for i in (0, 1, 2):
+            part = packed[i][low * CAP : high * CAP]
+            if i < 2:
+                xsend[g][i] = part
+            else:
+                ysend[g][...] = part
+    for g in range(2):
+        for i in (0, 1, 2):
+            x_copy(g, i).start()
+    dense(OPP, ZFIRST)
     for n in range(NOWN, count):
-        dense(n)
-        for direction in (0, 1):
-            chain_step(n, direction, 0)
-    for g in range(1, len(GROUPS)):
-        send_packed(g)
-    for n in range(NOWN):
-        dense(n)
+        for c in range(len(chains(n))):
+            chain_step(n, c, 0)
+    for g in range(2, len(GROUPS)):
+        for i in (0, 1, 2):
+            x_copy(g, i).start()
+    dense(OWN, W)
 
     number = counts[OWN]
-    for i in (0, 1):
+    for i in (0, 1, 2):
         meta[i].wait_recv()
-        number += spread(mrecv[i], i)
+        arrived = spread(mrecv[i], i)
+        if i < 2:
+            number += arrived
     fill_counts(0, number)
 
     for step in ORDER:
@@ -307,16 +335,21 @@
             number = jnp.maximum(jnp.sum(jnp.where(diag, number, 0.0), axis=1, keepdims=True), 1.0)
         for c in range(UNITS[n][2] // LANES):
             first_column = UNITS[n][1] + c * LANES
-            o = next(o for o in range(NOWN, count) if UNITS[o][1] <= first_column < UNITS[o][1] + UNITS[o][2])
-            other = orecv[o - NOWN][0:PROWS, first_column - UNITS[o][1] : first_column - UNITS[o][1] + LANES]
+            other = 0.0
+            for o in range(NOWN, count):
+                at = first_column - UNITS[o][1]
+                if 0 <= at < UNITS[o][2]:
+                    other = orecv[o - NOWN][0:PROWS, at : at + LANES]
             out[:, first_column : first_column + LANES] = (total[0:PROWS, c * LANES : (c + 1) * LANES] + other) / number
 
     remote(halo_out, halo_in, hs, hr.at[0], prv).wait_send()
     remote(msend, mrecv, ms, mr.at[0], at_x(1)).wait_send()
     for g in range(len(GROUPS)):
         remote(xsend[g], xrecv[g], xs.at[g], xr.at[g, 0], at_x(1)).wait_send()
+        x_copy(g, 2).wait_send()
     for n in range(count):
-        remote(ring[n], ring[n], rs.at[n], rr.at[n, 0], at_z(1)).wait_send()
+        sent = ring[n].at[:, rows_of(n)]
+        remote(sent, sent, rs.at[n], rr.at[n, 0], at_z(1)).wait_send()
     for n in range(NOWN, count):
         opp_copy(n).wait_send()
 
@@ -325,9 +358,10 @@
     anywhere = pl.BlockSpec(memory_space=pl.ANY)
     dma = pltpu.SemaphoreType.DMA
     vmem = pltpu.VMEM
-    blocks = [(rows, width) for _, _, width, rows in UNITS]
+    blocks = [(-(-rows // 8) * 8, width) for _, _, width, rows in UNITS]
     packs = [vmem((2, (high - low) * CAP, W), F32) for low, high in GROUPS]
-    places = [vmem((2, (high - low) * PROWS, (high - low) * CAP), BF16) for low, high in GROUPS]
+    places = [vmem((3, (high - low) * PROWS, (high - low) * CAP), BF16) for low, high in GROUPS]
+    sides = [vmem(((high - low) * CAP, W - ZFIRST), F32) for low, high in GROUPS]
     others = [vmem(block, F32) for block in blocks[NOWN:]]
     return pl.pallas_call(
         kernel,
@@ -348,18 +382,19 @@
             vmem((RO, W), BF16),
             vmem((RO, W), BF16),
             vmem((2, NZ * PROWS, RO), BF16),
-            vmem((2, NZ * CAP, RO), BF16),
+            vmem((3, NZ * CAP, RO), BF16),
             vmem((2, 8, W), F32),
             vmem((2, 8, W), F32),
-            vmem((2, 8, NZ * CAP), F32),
-            vmem((2, 8, NZ * CAP), F32),
+            vmem((3, 8, NZ * CAP), F32),
+            vmem((3, 8, NZ * CAP), F32),
             dma((9,)),
             dma(()),
             dma((2,)),
             dma(()),
-            dma((2,)),
+            dma((3,)),
             dma((len(GROUPS),)),
-            dma((len(GROUPS), 2)),
+            dma((len(GROUPS),)),
+            dma((len(GROUPS), 3)),
             dma((len(UNITS),)),
             dma((len(UNITS), NM)),
             dma((len(UNITS) - NOWN,)),
@@ -371,7 +406,9 @@
         + others
         + packs
         + packs
-        + places,
+        + places
+        + sides
+        + sides,
         compiler_params=pltpu.CompilerParams(collective_id=0, has_side_effects=True),
     )(
         exposure,

time: 52.5 us -> 47.9 us (0.912)
  Pallas kernels: 51.7 us -> 47.1 us
    pallas_call x1, Pallas kernels: 51.7 us -> 47.1 us  [on_device(): pl.pallas_call(kernel, out_shape=vmem((PROWS, W), F32), in_specs=[anywher...]
where the time goes in v3:
time: 47.9 us; the launch traced here: 47.7 us
  Pallas kernels  47.1 us (98%)
  local copies, waits for them, and re-layouts  0.63 us (1%)
    pallas_call x1, Pallas kernels, on_device(): pl.pallas_call(kernel, out_shape=vmem((PROWS, W), F32), in_specs=[anywher...  47.1 us

profile of v3, /device:TPU:24, one launch (start us, length us, event | category | flops | bytes accessed | tf_op | source)
XLA Modules:
  0.0 47.7 jit_solution(8166929647641428926)
XLA Ops:
  0.0 47.1 %shard_map.73 = f32[32,512]{1,0:T(8,128)S(1)} custom-call(f32[1024,512]{1,0:T(8,128)} %expo.1, bf16[1,15]{1,0:T(2,128)(2,1)} %taps_hbm.1, bf16[512,512]{1,0:T(8,128)(2,1)} %cw_hbm.1, bf16[512,1024]{1,0:T(8,128)(2,1)} %rw_hbm.1, s32[1,512]{1,0:T(1,128)} %bitcast.3, s32[1,512]{1,0:T(1,128)} %bitcast.4, s32[1,64]{1,0:T(1,128)} %bitcast.5), custom_call_target="tpu_custom_call" | custom-call | tf_op jit(solution)/shard_map/pallas_call | solution.py:366
  47.1 0.6 %copy.9 = f32[32,512]{1,0:T(8,128)} copy(f32[32,512]{1,0:T(8,128)S(1)} %shard_map.73) | data formatting | bytes 131072

commit v4 on v3

--- a/solution.py
+++ b/solution.py
@@ -33,20 +33,21 @@
 )
 NOWN = sum(u[0] == OWN for u in UNITS)
 ZFIRST = 256
+XTILES = 3 * NC - ZFIRST // LANES
 NEAR = (2, 2)
-SPOT = (15, 13, 11, 9, 7, 5, 3, 1, 0, 2, 4, 6, 8, 10, 12, 14)
-GROUPS = ((0, 2), (2, 4), (4, 6), (6, 8), (8, 10), (10, 12), (12, 14), (14, 16))
+SPOT = (15, 13, 7, 11, 9, 5, 3, 1, 0, 2, 4, 6, 10, 12, 8, 14)
+GROUPS = ((0, 1), (1, 3), (3, 5), (5, 7), (7, 9), (9, 11), (11, 13), (13, 16))
 ORDER = (
-    (4, 0, 1), (4, 2, 1), (4, 1, 1), (4, 3, 1), (5, 2, 1), (5, 0, 1), (5, 1, 1), (5, 3, 1), ("x", 0), (0, 0, 0),
-    (1, 2, 0), (2, 0, 0), (3, 2, 0), (1, 0, 0), (3, 0, 0), (4, 0, 2), (4, 2, 2), ("x", 1), (0, 2, 0), (2, 2, 0),
-    (5, 0, 2), (5, 2, 2), (1, 2, 1), (0, 0, 1), (3, 2, 1), (2, 0, 1), (1, 0, 1), ("x", 2), (3, 0, 1), (4, 0, 3),
-    (4, 2, 3), (0, 2, 1), (5, 0, 3), (2, 2, 1), (5, 2, 3), ("x", 3), (1, 2, 2), (0, 0, 2), (3, 2, 2), (2, 0, 2),
-    (1, 0, 2), (3, 0, 2), (4, 0, 4), (4, 2, 4), ("x", 4), (0, 2, 2), (5, 0, 4), (2, 2, 2), (5, 2, 4), (1, 2, 3),
-    (0, 0, 3), (3, 2, 3), (2, 0, 3), (1, 0, 3), ("x", 5), (0, 1, 0), (1, 1, 0), (2, 1, 0), (3, 1, 0), (3, 0, 3),
-    (4, 0, 5), (0, 2, 3), (2, 2, 3), ("x", 6), (0, 3, 0), (1, 3, 0), (2, 3, 0), (3, 3, 0), (0, 0, 4), (5, 2, 5),
-    (2, 0, 4), (1, 2, 4), (1, 0, 4), (3, 2, 4), (0, 1, 1), (1, 1, 1), (2, 1, 1), ("x", 7), (3, 1, 1), (3, 0, 4),
-    (0, 2, 4), (2, 2, 4), (0, 3, 1), (1, 3, 1), (0, 0, 5), (2, 3, 1), (2, 0, 5), (3, 3, 1), ("o", 4), (1, 2, 5),
-    (3, 2, 5), ("o", 5),
+    (4, 0, 1), (4, 2, 1), (4, 1, 1), (4, 3, 1), ("x", 0), (5, 2, 1), (0, 0, 0), (1, 2, 0), (2, 0, 0), (3, 2, 0),
+    (5, 0, 1), (5, 1, 1), (5, 3, 1), ("x", 1), (0, 2, 0), (1, 0, 0), (2, 2, 0), (3, 0, 0), (4, 0, 2), (4, 2, 2),
+    (5, 2, 2), (0, 0, 1), (1, 2, 1), (2, 0, 1), (3, 2, 1), (5, 0, 2), ("x", 2), (1, 0, 1), (0, 2, 1), (3, 0, 1),
+    (2, 2, 1), (4, 0, 3), (4, 2, 3), ("x", 3), (5, 2, 3), (0, 0, 2), (1, 2, 2), (2, 0, 2), (3, 2, 2), (5, 0, 3),
+    ("x", 4), (0, 1, 0), (1, 0, 2), (0, 3, 0), (0, 2, 2), (1, 1, 0), (1, 3, 0), (2, 1, 0), (2, 3, 0), (3, 1, 0),
+    (3, 3, 0), (3, 0, 2), (2, 2, 2), (4, 0, 4), (4, 2, 4), (5, 2, 4), (0, 0, 3), (1, 2, 3), (2, 0, 3), (3, 2, 3),
+    (5, 0, 4), ("x", 5), (1, 0, 3), (0, 2, 3), ("x", 6), (3, 0, 3), (2, 2, 3), (4, 0, 5), (0, 0, 4), (2, 0, 4),
+    (5, 2, 5), (1, 2, 4), (3, 2, 4), ("x", 7), (1, 0, 4), (0, 1, 1), (0, 3, 1), (0, 2, 4), (1, 1, 1), (1, 3, 1),
+    (2, 1, 1), (2, 3, 1), (3, 1, 1), (3, 3, 1), (3, 0, 4), (2, 2, 4), (0, 0, 5), (2, 0, 5), (1, 2, 5), (3, 2, 5),
+    ("o", 4), ("o", 5),
 )
 
 
@@ -85,7 +86,7 @@
 def kernel(
     expo, taps_hbm, cw_hbm, rw_hbm, patch_hbm, prow_hbm, owner_hbm, out,
     ex, strips, taps, cw, rw, patch, prow, owner, mat, corr, ybuf, wbuf, sel, pack, halo_out, halo_in,
-    msend, mrecv, in_sem, hs, hr, ms, mr, xs, ys, xr, rs, rr, os, oR, *buffers,
+    msend, mrecv, xsend, xrecv, in_sem, hs, hr, ms, mr, xs, xr, rs, rr, os, oR, *buffers,
 ):
     buffers = list(buffers)
 
@@ -94,8 +95,7 @@
 
     count = len(UNITS)
     acc, ring, osend, orecv = take(count), take(count), take(count - NOWN), take(count - NOWN)
-    xsend, xrecv, place = take(len(GROUPS)), take(len(GROUPS)), take(len(GROUPS))
-    ysend, yrecv = take(len(GROUPS)), take(len(GROUPS))
+    place = take(len(GROUPS))
     e = lax.axis_index("exp")
     x, z = e // NZ, lax.rem(e, NZ)
 
@@ -153,8 +153,8 @@
     halo_out[1] = jnp.broadcast_to(last, (8, W))
     pl.semaphore_wait(barrier, len(peers))
     halo = [
-        remote(halo_out.at[0], halo_in.at[0], hs, hr.at[0], prv),
-        remote(halo_out.at[1], halo_in.at[1], hs, hr.at[1], nxt),
+        remote(halo_out.at[0], halo_in.at[0], hs, hr, prv),
+        remote(halo_out.at[1], halo_in.at[1], hs, hr, nxt),
     ]
     for copy in halo:
         copy.start()
@@ -180,7 +180,7 @@
         to = dest_x == lax.rem(x + k, NX)
         pack[i] = equal(iota((NZ * CAP, RO), 0), jnp.where(to, slot, -1))
         msend[i] = nt(prow_row, pack[i])
-        meta.append(remote(msend.at[i], mrecv.at[i], ms, mr.at[i], at_x(k)))
+        meta.append(remote(msend.at[i], mrecv.at[i], ms, mr, at_x(k)))
         meta[-1].start()
 
     oz = equal(iota((NZ, RO), 0), spot)
@@ -206,15 +206,22 @@
 
     piece_load.wait()
     row_load.wait()
-    for copy in halo:
-        copy.wait_recv()
+    remote(halo_out, halo_in, hs, hr, prv).wait_recv()
     off_next = last - halo_in[0][0:1]
     off_prev = halo_in[1][0:1] - first
     shift = -0.5 * off_next + 0.5 * off_prev
 
+    def x_part(g, i):
+        low, high = GROUPS[g]
+        return pl.ds(i * NC, NC if i < 2 else XTILES - 2 * NC), pl.ds(low * CAP, (high - low) * CAP)
+
     def x_copy(g, i):
-        source, target = (xsend[g].at[i], xrecv[g].at[i]) if i < 2 else (ysend[g], yrecv[g])
-        return remote(source, target, (xs if i < 2 else ys).at[g], xr.at[g, i], at_x(SIDES[i]))
+        part = x_part(g, i)
+        return remote(xsend.at[part], xrecv.at[part], xs, xr.at[g], at_x(SIDES[i]))
+
+    def x_wait(g):
+        part = xrecv.at[:, x_part(g, 0)[1]]
+        remote(part, part, xs, xr.at[g], at_x(1)).wait_recv()
 
     def rows_of(n):
         return pl.ds(0, UNITS[n][3])
@@ -262,16 +269,19 @@
 
     def take_packed(g):
         low, high = GROUPS[g]
-        for i in (0, 1, 2):
-            x_copy(g, i).wait_recv()
+        slots = slice(low * CAP, high * CAP)
+        x_wait(g)
         for n in range(NOWN):
             shape = (high - low, PROWS, UNITS[n][2])
             total = acc[n][low:high, 0:PROWS].reshape(shape[0] * PROWS, shape[2])
-            for i in (0, 1):
-                total += mm(place[g][i], xrecv[g][i, :, columns(n)].astype(BF16))
-            if UNITS[n][1] >= ZFIRST:
-                part = slice(UNITS[n][1] - ZFIRST, UNITS[n][1] - ZFIRST + UNITS[n][2])
-                total += mm(place[g][2], yrecv[g][:, part].astype(BF16))
+            first_tile, tiles = UNITS[n][1] // LANES, UNITS[n][2] // LANES
+            for i in (0, 1, 2):
+                if i == 2 and UNITS[n][1] < ZFIRST:
+                    continue
+                at = i * NC + first_tile - (ZFIRST // LANES if i == 2 else 0)
+                arrived = [xrecv[at + tile, slots] for tile in range(tiles)]
+                arrived = arrived[0] if tiles == 1 else jnp.concatenate(arrived, axis=1)
+                total += mm(place[g][i], arrived.astype(BF16))
             acc[n][low:high, 0:PROWS] = total.reshape(shape)
 
     def fill_counts(n, number):
@@ -290,13 +300,9 @@
     ybuf[...] = mm(rw[...], corr[...]).astype(BF16)
     wbuf[...] = mm(ybuf[...], mat[...]).astype(BF16)
     packed = [mm(pack[i], wbuf[...] if i < 2 else wbuf[:, ZFIRST:]) for i in (0, 1, 2)]
-    for g, (low, high) in enumerate(GROUPS):
-        for i in (0, 1, 2):
-            part = packed[i][low * CAP : high * CAP]
-            if i < 2:
-                xsend[g][i] = part
-            else:
-                ysend[g][...] = part
+    for i in (0, 1, 2):
+        for tile in range(NC if i < 2 else XTILES - 2 * NC):
+            xsend[i * NC + tile] = packed[i][:, tile * LANES : (tile + 1) * LANES]
     for g in range(2):
         for i in (0, 1, 2):
             x_copy(g, i).start()
@@ -310,8 +316,8 @@
     dense(OWN, W)
 
     number = counts[OWN]
+    remote(msend, mrecv, ms, mr, at_x(1)).wait_recv()
     for i in (0, 1, 2):
-        meta[i].wait_recv()
         arrived = spread(mrecv[i], i)
         if i < 2:
             number += arrived
@@ -342,11 +348,9 @@
                     other = orecv[o - NOWN][0:PROWS, at : at + LANES]
             out[:, first_column : first_column + LANES] = (total[0:PROWS, c * LANES : (c + 1) * LANES] + other) / number
 
-    remote(halo_out, halo_in, hs, hr.at[0], prv).wait_send()
-    remote(msend, mrecv, ms, mr.at[0], at_x(1)).wait_send()
-    for g in range(len(GROUPS)):
-        remote(xsend[g], xrecv[g], xs.at[g], xr.at[g, 0], at_x(1)).wait_send()
-        x_copy(g, 2).wait_send()
+    remote(halo_out, halo_in, hs, hr, prv).wait_send()
+    remote(msend, mrecv, ms, mr, at_x(1)).wait_send()
+    remote(xsend, xrecv, xs, xr.at[0], at_x(1)).wait_send()
     for n in range(count):
         sent = ring[n].at[:, rows_of(n)]
         remote(sent, sent, rs.at[n], rr.at[n, 0], at_z(1)).wait_send()
@@ -359,9 +363,7 @@
     dma = pltpu.SemaphoreType.DMA
     vmem = pltpu.VMEM
     blocks = [(-(-rows // 8) * 8, width) for _, _, width, rows in UNITS]
-    packs = [vmem((2, (high - low) * CAP, W), F32) for low, high in GROUPS]
     places = [vmem((3, (high - low) * PROWS, (high - low) * CAP), BF16) for low, high in GROUPS]
-    sides = [vmem(((high - low) * CAP, W - ZFIRST), F32) for low, high in GROUPS]
     others = [vmem(block, F32) for block in blocks[NOWN:]]
     return pl.pallas_call(
         kernel,
@@ -387,14 +389,15 @@
             vmem((2, 8, W), F32),
             vmem((3, 8, NZ * CAP), F32),
             vmem((3, 8, NZ * CAP), F32),
+            vmem((XTILES, NZ * CAP, LANES), F32),
+            vmem((XTILES, NZ * CAP, LANES), F32),
             dma((9,)),
             dma(()),
-            dma((2,)),
             dma(()),
-            dma((3,)),
+            dma(()),
+            dma(()),
+            dma(()),
             dma((len(GROUPS),)),
-            dma((len(GROUPS),)),
-            dma((len(GROUPS), 3)),
             dma((len(UNITS),)),
             dma((len(UNITS), NM)),
             dma((len(UNITS) - NOWN,)),
@@ -404,11 +407,7 @@
         + [vmem((NM, *block), F32) for block in blocks]
         + others
         + others
-        + packs
-        + packs
-        + places
-        + sides
-        + sides,
+        + places,
         compiler_params=pltpu.CompilerParams(collective_id=0, has_side_effects=True),
     )(
         exposure,

time: 47.9 us -> 46.1 us (0.962)
  Pallas kernels: 47.1 us -> 45.4 us
    pallas_call x1, Pallas kernels: 47.1 us -> 45.4 us  [on_device(): pl.pallas_call(kernel, out_shape=vmem((PROWS, W), F32), in_specs=[anywher...]
where the time goes in v4:
time: 46.1 us; the launch traced here: 46 us
  Pallas kernels  45.4 us (98%)
  local copies, waits for them, and re-layouts  0.63 us (1%)
    pallas_call x1, Pallas kernels, on_device(): pl.pallas_call(kernel, out_shape=vmem((PROWS, W), F32), in_specs=[anywher...  45.4 us

profile of v4, /device:TPU:24, one launch (start us, length us, event | category | flops | bytes accessed | tf_op | source)
XLA Modules:
  0.0 46.0 jit_solution(15189115416230496196)
XLA Ops:
  0.0 45.4 %shard_map.73 = f32[32,512]{1,0:T(8,128)S(1)} custom-call(f32[1024,512]{1,0:T(8,128)} %expo.1, bf16[1,15]{1,0:T(2,128)(2,1)} %taps_hbm.1, bf16[512,512]{1,0:T(8,128)(2,1)} %cw_hbm.1, bf16[512,1024]{1,0:T(8,128)(2,1)} %rw_hbm.1, s32[1,512]{1,0:T(1,128)} %bitcast.3, s32[1,512]{1,0:T(1,128)} %bitcast.4, s32[1,64]{1,0:T(1,128)} %bitcast.5), custom_call_target="tpu_custom_call" | custom-call | tf_op jit(solution)/shard_map/pallas_call | solution.py:368
  45.4 0.6 %copy.9 = f32[32,512]{1,0:T(8,128)} copy(f32[32,512]{1,0:T(8,128)S(1)} %shard_map.73) | data formatting | bytes 131072
